TPU v7x, 32 devices: a whole 2x2x4 slice. The times are simulated.
32 devices in a mesh: band: 2 (over y), mesh: 16 (over z, x, core).
Axes of the slice: x: 2, y: 2, z: 4, core: 2. Of those that a mesh axis runs over, the one named last changes fastest.
Arguments:
- psi: bfloat16 [16, 1536, 1536], P('mesh', 'band'), may hold values from -6 to 6
- ritz: bfloat16 [1536, 1536], replicated, may hold values from -0.15625 to 0.15625
- cell_ham: bfloat16 [16, 4, 512, 512], P('mesh'), may hold values from -0.25 to 0.25
- cell_nodes: int32 [16, 4, 512], P('mesh'), may hold values from 0 to 1535, as said below
- face_nodes: int32 [16, 4, 256], P('mesh'), may hold values from 0 to 1535, as said below
Outputs:
- filtered: bfloat16 [16, 1536, 1536], P('mesh', None, 'band')
Inputs may be any that keep to these rules, and one draw needn't show every extreme that they name: `cell_nodes`: each row of 512 entries names distinct local nodes, and every local node lies in some cell of its partition. `face_nodes`: the 1024 entries of one partition name distinct local nodes.
All inputs are finite; a program needn't handle non-finite values.
Results may differ from a plain program's by a relative error of at most 0.0058.
Values may be sent and summed in bfloat16 or wider, within the bound.
A program may use at most 64 MiB of HBM per device.

v0:
```python
import jax
import jax.numpy as jnp
from jax import lax
from jax.sharding import PartitionSpec as P

GRID_W = 4


def passed_along(value, axis, by):
    count = lax.axis_size(axis)
    return lax.ppermute(value, axis, [(i, (i + by) % count) for i in range(count)])


def operate(vectors, cell_ham, nodes, faces):
    count = vectors.shape[0]
    width = vectors.shape[1]
    empty = jnp.zeros((count, width), jnp.float32)
    picked = vectors[nodes]
    products = jnp.einsum("cij,cjb->cib", cell_ham, picked, preferred_element_type=jnp.float32)
    summed = empty.at[nodes.reshape(-1)].add(products.reshape(-1, width))
    rounded = summed.astype(jnp.bfloat16)
    flat_faces = faces.reshape(-1)
    blocks = rounded[flat_faces].reshape(4, -1, width)
    arrived = []
    for send_dir, offset in ((1, 1), (0, -1)):
        arrived.append(passed_along(blocks[send_dir], "mesh", offset))
    for send_dir, offset in ((3, GRID_W), (2, -GRID_W)):
        arrived.append(passed_along(blocks[send_dir], "mesh", offset))
    incoming = jnp.stack(arrived).astype(jnp.float32).reshape(-1, width)
    return summed.at[flat_faces].add(incoming)


def local(psi, ritz, cell_ham, cell_nodes, face_nodes):
    own_rows = psi[0]
    rotated_rows = jnp.dot(own_rows, ritz, preferred_element_type=jnp.float32).astype(jnp.bfloat16)
    rotated = lax.all_to_all(rotated_rows, "band", split_axis=1, concat_axis=0, tiled=True)
    hams = cell_ham[0]
    nodes = cell_nodes[0]
    faces = face_nodes[0]
    applied = operate(rotated, hams, nodes, faces)
    rotated_f = rotated.astype(jnp.float32)
    first = ((applied - 0.25 * rotated_f) / 2.0).astype(jnp.bfloat16)
    applied_next = operate(first, hams, nodes, faces)
    filtered = 2.0 * (applied_next - 0.25 * first.astype(jnp.float32)) / 2.0 - rotated_f
    return filtered.astype(jnp.bfloat16)[None]


def solution(mesh):
    return jax.shard_map(
        local,
        mesh=mesh,
        in_specs=(
            P("mesh", "band", None),
            P(),
            P("mesh", None, None, None),
            P("mesh", None, None),
            P("mesh", None, None),
        ),
        out_specs=P("mesh", None, "band"),
        check_vma=False,
    )
```

profile of v0, /device:TPU:0, one launch (start us, length us, event | category | flops | bytes accessed | tf_op | source)
XLA Modules:
  0.0 232.1 jit_solution(12796402053414573186)
XLA Ops:
  0.0 0.0 copy-start
  0.0 1.7 copy-done
  1.7 6.3 %convolution_convert_fusion = bf16[768,1536]{1,0:T(8,128)(2,1)S(1)} fusion(bf16[1536,1536]{1,0:T(8,128)(2,1)} %param.6, bf16[1,768,1536]{2,1,0:T(8,128)(2,1)S(1)} %copy-done), kind=kOutput, calls=%fused_computation.14 | convolution fusion | flops 3625058304 | bytes 9437184 | tf_op jit(solution)/shard_map/dot_general | solution.py:35
  8.0 1.6 copy.13
  9.6 0.0 copy-start.1
  9.6 0.0 copy-start.2
  9.6 5.0 %all-to-all-start = ((bf16[768,2,768]{2,0,1:T(8,128)(2,1)}), bf16[768,2,768]{2,0,1:T(8,128)(2,1)}, u32[]{:S(2)}, u32[]{:S(2)}) async-start(bf16[768,2,768]{2,0,1:T(8,128)(2,1)} %bitcast.58), calls=%async_computation | async-start | bytes 4718592 | tf_op jit(solution)/shard_map/all_to_all | solution.py:36
  14.6 0.0 copy-done.1
  14.7 0.0 copy-done.2
  14.8 29.2 %all-to-all-done = bf16[768,2,768]{2,0,1:T(8,128)(2,1)} async-done(((bf16[768,2,768]{2,0,1:T(8,128)(2,1)}), bf16[768,2,768]{2,0,1:T(8,128)(2,1)}, u32[]{:S(2)}, u32[]{:S(2)}) %all-to-all-start) | async-done | bytes 2359328 | tf_op jit(solution)/shard_map/all_to_all | solution.py:36
  43.9 12.1 %gather_fusion = bf16[2048,768]{1,0:T(8,128)(2,1)} fusion(bf16[1536,768]{1,0:T(8,128)(2,1)} %bitcast.3, s32[2048]{0:T(1024)S(1)} %broadcast_clamp_fusion), kind=kCustom, calls=%fused_computation | custom fusion | bytes 6299648 | tf_op jit(solution)/shard_map/gather | solution.py:18
  56.0 7.0 %fusion.14 = f32[4,768,512]{1,2,0:T(8,128)} fusion(bf16[4,512,768]{2,1,0:T(8,128)(2,1)} %bitcast.57, bf16[1,4,512,512]{3,2,1,0:T(8,128)(2,1)} %param.7), kind=kOutput, calls=%fused_computation.26 | convolution fusion | flops 1610612736 | bytes 11534336 | tf_op jit(solution)/shard_map/cij,cjb->cib/dot_general | solution.py:19
  63.0 17.0 %scatter_custom_fusion = f32[1536,768]{1,0:T(8,128)} fusion(s32[2048]{0:T(1024)S(1)} %bitcast.79, f32[2048,768]{1,0:T(8,128)} %bitcast.62, f32[]{:T(128)} %constant.5.clone.1), kind=kCustom, calls=%fused_computation.24 | custom fusion | flops 1572864 | bytes 4719104 | tf_op jit(solution)/shard_map/scatter-add | solution.py:20
  79.9 4.0 %convert_element_type.36 = bf16[1536,768]{1,0:T(8,128)(2,1)} convert(f32[1536,768]{1,0:T(8,128)} %scatter_custom_fusion) | non-fusion elementwise | flops 1179648 | bytes 7077888 | tf_op jit(solution)/shard_map/convert_element_type | solution.py:21
  83.9 7.5 %gather_fusion.1 = bf16[1024,768]{1,0:T(8,128)(2,1)} fusion(bf16[1536,768]{1,0:T(8,128)(2,1)} %convert_element_type.36, s32[1024]{0:T(1024)S(1)} %broadcast_clamp_fusion.1), kind=kCustom, calls=%fused_computation.1 | custom fusion | bytes 3149824 | tf_op jit(solution)/shard_map/gather | solution.py:23
  91.5 1.5 fusion.20
  92.9 0.1 collective-permute-start
  93.0 1.8 collective-permute-start.2
  94.8 4.1 %collective-permute-start.1 = (bf16[256,768]{1,0:T(8,128)(2,1)S(1)}, bf16[256,768]{1,0:T(8,128)(2,1)S(1)}, u32[]{:S(2)}, u32[]{:S(2)}) collective-permute-start(bf16[256,768]{1,0:T(8,128)(2,1)S(1)} %get-tuple-element.11), channel_id=1, source_target_pairs={{0,15},{1,0},{2,1},{3,2},{4,3},{5,4},{6,5},{7,6},{8,7},{9,8},{10,9... | collective-permute-start | bytes 1179656 | tf_op jit(solution)/shard_map/ppermute | solution.py:11
  98.9 0.5 collective-permute-start.3
  99.4 7.0 %collective-permute-done = bf16[256,768]{1,0:T(8,128)(2,1)S(1)} collective-permute-done((bf16[256,768]{1,0:T(8,128)(2,1)S(1)}, bf16[256,768]{1,0:T(8,128)(2,1)S(1)}, u32[]{:S(2)}, u32[]{:S(2)}) %collective-permute-start) | collective-permute-done | bytes 393248 | tf_op jit(solution)/shard_map/ppermute | solution.py:11
  106.3 0.0 collective-permute-done.2
  106.3 5.8 %collective-permute-done.1 = bf16[256,768]{1,0:T(8,128)(2,1)S(1)} collective-permute-done((bf16[256,768]{1,0:T(8,128)(2,1)S(1)}, bf16[256,768]{1,0:T(8,128)(2,1)S(1)}, u32[]{:S(2)}, u32[]{:S(2)}) %collective-permute-start.1) | collective-permute-done | bytes 393248 | tf_op jit(solution)/shard_map/ppermute | solution.py:11
  112.2 7.3 %collective-permute-done.3 = bf16[256,768]{1,0:T(8,128)(2,1)S(1)} collective-permute-done((bf16[256,768]{1,0:T(8,128)(2,1)S(1)}, bf16[256,768]{1,0:T(8,128)(2,1)S(1)}, u32[]{:S(2)}, u32[]{:S(2)}) %collective-permute-start.3) | collective-permute-done | bytes 393248 | tf_op jit(solution)/shard_map/ppermute | solution.py:11
  119.5 1.3 pad_maximum_fusion
  120.8 12.4 %scatter_custom_fusion.1 = f32[1536,768]{1,0:T(8,128)} fusion(f32[1536,768]{1,0:T(8,128)} %scatter_custom_fusion, s32[1024]{0:T(1024)S(1)} %bitcast.76, bf16[1024,768]{1,0:T(8,128)(2,1)} %bitcast.60), kind=kCustom, calls=%fused_computation.17 | custom fusion | flops 1572864 | bytes 6291456 | tf_op jit(solution)/shard_map/scatter-add | solution.py:30
  133.2 5.2 %fusion.2 = bf16[1536,768]{1,0:T(8,128)(2,1)} fusion(f32[1536,768]{1,0:T(8,128)} %scatter_custom_fusion.1, bf16[768,2,768]{2,0,1:T(8,128)(2,1)} %all-to-all-done), kind=kLoop, calls=%fused_computation.12 | loop fusion | flops 5898240 | bytes 9437184 | tf_op jit(solution)/shard_map/convert_element_type | solution.py:42
  138.4 12.1 %gather_fusion.2 = bf16[2048,768]{1,0:T(8,128)(2,1)} fusion(bf16[1536,768]{1,0:T(8,128)(2,1)} %fusion.2, s32[2048]{0:T(1024)S(1)} %broadcast_clamp_fusion), kind=kCustom, calls=%fused_computation.2 | custom fusion | bytes 6299648 | tf_op jit(solution)/shard_map/gather | solution.py:18
  150.5 7.0 %fusion.16 = f32[4,768,512]{1,2,0:T(8,128)} fusion(bf16[4,512,768]{2,1,0:T(8,128)(2,1)} %bitcast.56, bf16[1,4,512,512]{3,2,1,0:T(8,128)(2,1)} %param.7), kind=kOutput, calls=%fused_computation.28 | convolution fusion | flops 1610612736 | bytes 11534336 | tf_op jit(solution)/shard_map/cij,cjb->cib/dot_general | solution.py:19
  157.5 17.0 %scatter_custom_fusion.2 = f32[1536,768]{1,0:T(8,128)} fusion(s32[2048]{0:T(1024)S(1)} %bitcast.80, f32[2048,768]{1,0:T(8,128)} %bitcast.61, f32[]{:T(128)} %constant.5.clone.1), kind=kCustom, calls=%fused_computation.22 | custom fusion | flops 1572864 | bytes 4719104 | tf_op jit(solution)/shard_map/scatter-add | solution.py:20
  174.4 4.0 %convert_element_type.41 = bf16[1536,768]{1,0:T(8,128)(2,1)} convert(f32[1536,768]{1,0:T(8,128)} %scatter_custom_fusion.2) | non-fusion elementwise | flops 1179648 | bytes 7077888 | tf_op jit(solution)/shard_map/convert_element_type | solution.py:21
  178.4 7.6 %gather_fusion.3 = bf16[1024,768]{1,0:T(8,128)(2,1)} fusion(bf16[1536,768]{1,0:T(8,128)(2,1)} %convert_element_type.41, s32[1024]{0:T(1024)S(1)} %broadcast_clamp_fusion.1), kind=kCustom, calls=%fused_computation.3 | custom fusion | bytes 3149824 | tf_op jit(solution)/shard_map/gather | solution.py:23
  186.0 1.5 fusion.19
  187.4 0.1 collective-permute-start.4
  187.5 0.6 collective-permute-start.6
  188.1 4.1 %collective-permute-start.5 = (bf16[256,768]{1,0:T(8,128)(2,1)S(1)}, bf16[256,768]{1,0:T(8,128)(2,1)S(1)}, u32[]{:S(2)}, u32[]{:S(2)}) collective-permute-start(bf16[256,768]{1,0:T(8,128)(2,1)S(1)} %get-tuple-element.7), channel_id=1, source_target_pairs={{0,15},{1,0},{2,1},{3,2},{4,3},{5,4},{6,5},{7,6},{8,7},{9,8},{10,9... | collective-permute-start | bytes 1179656 | tf_op jit(solution)/shard_map/ppermute | solution.py:11
  192.2 1.5 collective-permute-start.7
  193.7 8.0 %collective-permute-done.4 = bf16[256,768]{1,0:T(8,128)(2,1)S(1)} collective-permute-done((bf16[256,768]{1,0:T(8,128)(2,1)S(1)}, bf16[256,768]{1,0:T(8,128)(2,1)S(1)}, u32[]{:S(2)}, u32[]{:S(2)}) %collective-permute-start.4) | collective-permute-done | bytes 393248 | tf_op jit(solution)/shard_map/ppermute | solution.py:11
  201.7 0.0 collective-permute-done.6
  201.7 4.2 %collective-permute-done.5 = bf16[256,768]{1,0:T(8,128)(2,1)S(1)} collective-permute-done((bf16[256,768]{1,0:T(8,128)(2,1)S(1)}, bf16[256,768]{1,0:T(8,128)(2,1)S(1)}, u32[]{:S(2)}, u32[]{:S(2)}) %collective-permute-start.5) | collective-permute-done | bytes 393248 | tf_op jit(solution)/shard_map/ppermute | solution.py:11
  206.0 6.4 %collective-permute-done.7 = bf16[256,768]{1,0:T(8,128)(2,1)S(1)} collective-permute-done((bf16[256,768]{1,0:T(8,128)(2,1)S(1)}, bf16[256,768]{1,0:T(8,128)(2,1)S(1)}, u32[]{:S(2)}, u32[]{:S(2)}) %collective-permute-start.7) | collective-permute-done | bytes 393248 | tf_op jit(solution)/shard_map/ppermute | solution.py:11
  212.4 1.4 pad_maximum_fusion.1
  213.7 12.4 %scatter_custom_fusion.3 = f32[1536,768]{1,0:T(8,128)} fusion(f32[1536,768]{1,0:T(8,128)} %scatter_custom_fusion.2, s32[1024]{0:T(1024)S(1)} %bitcast.77, bf16[1024,768]{1,0:T(8,128)(2,1)} %bitcast.59), kind=kCustom, calls=%fused_computation.15 | custom fusion | flops 1572864 | bytes 6291456 | tf_op jit(solution)/shard_map/scatter-add | solution.py:30
  226.1 6.0 %fusion.8 = bf16[1,1536,768]{2,1,0:T(8,128)(2,1)} fusion(f32[1536,768]{1,0:T(8,128)} %scatter_custom_fusion.3, bf16[1536,768]{1,0:T(8,128)(2,1)} %fusion.2, bf16[768,2,768]{2,0,1:T(8,128)(2,1)} %all-to-all-done), kind=kLoop, calls=%fused_computation.19 | loop fusion | flops 7077888 | bytes 11796480 | tf_op jit(solution)/shard_map/broadcast_in_dim | solution.py:45
  (8 shorter events, 0.1 us)
Async XLA Ops:
  0.0 1.7 copy-start
  9.6 5.1 %copy-start.1 = (s32[1,4,512]{2,1,0:T(4,128)S(1)}, s32[1,4,512]{2,1,0:T(4,128)}, u32[]{:S(2)}) copy-start(s32[1,4,512]{2,1,0:T(4,128)} %param.8) | copy-start | bytes 24580
  9.6 5.1 %copy-start.2 = (s32[1,4,256]{2,1,0:T(4,128)S(1)}, s32[1,4,256]{2,1,0:T(4,128)}, u32[]{:S(2)}) copy-start(s32[1,4,256]{2,1,0:T(4,128)} %param.9) | copy-start | bytes 12292
  9.6 34.4 %all-to-all-start = ((bf16[768,2,768]{2,0,1:T(8,128)(2,1)}), bf16[768,2,768]{2,0,1:T(8,128)(2,1)}, u32[]{:S(2)}, u32[]{:S(2)}) async-start(bf16[768,2,768]{2,0,1:T(8,128)(2,1)} %bitcast.58), calls=%async_computation | async-start | bytes 4718592 | tf_op jit(solution)/shard_map/all_to_all | solution.py:36
  92.9 13.4 %collective-permute-start = (bf16[256,768]{1,0:T(8,128)(2,1)S(1)}, bf16[256,768]{1,0:T(8,128)(2,1)S(1)}, u32[]{:S(2)}, u32[]{:S(2)}) collective-permute-start(bf16[256,768]{1,0:T(8,128)(2,1)S(1)} %get-tuple-element.9), channel_id=1, source_target_pairs={{0,1},{1,2},{2,3},{3,4},{4,5},{5,6},{6,7},{7,8},{8,9},{9,10},{10,1... | collective-permute-start | bytes 1179656 | tf_op jit(solution)/shard_map/ppermute | solution.py:11
  93.0 13.4 %collective-permute-start.2 = (bf16[256,768]{1,0:T(8,128)(2,1)S(1)}, bf16[256,768]{1,0:T(8,128)(2,1)S(1)}, u32[]{:S(2)}, u32[]{:S(2)}) collective-permute-start(bf16[256,768]{1,0:T(8,128)(2,1)S(1)} %get-tuple-element.10), channel_id=1, source_target_pairs={{0,4},{1,5},{2,6},{3,7},{4,8},{5,9},{6,10},{7,11},{8,12},{9,13},{1... | collective-permute-start | bytes 1179656 | tf_op jit(solution)/shard_map/ppermute | solution.py:11
  94.8 17.4 %collective-permute-start.1 = (bf16[256,768]{1,0:T(8,128)(2,1)S(1)}, bf16[256,768]{1,0:T(8,128)(2,1)S(1)}, u32[]{:S(2)}, u32[]{:S(2)}) collective-permute-start(bf16[256,768]{1,0:T(8,128)(2,1)S(1)} %get-tuple-element.11), channel_id=1, source_target_pairs={{0,15},{1,0},{2,1},{3,2},{4,3},{5,4},{6,5},{7,6},{8,7},{9,8},{10,9... | collective-permute-start | bytes 1179656 | tf_op jit(solution)/shard_map/ppermute | solution.py:11
  98.9 20.6 %collective-permute-start.3 = (bf16[256,768]{1,0:T(8,128)(2,1)S(1)}, bf16[256,768]{1,0:T(8,128)(2,1)S(1)}, u32[]{:S(2)}, u32[]{:S(2)}) collective-permute-start(bf16[256,768]{1,0:T(8,128)(2,1)S(1)} %get-tuple-element.12), channel_id=1, source_target_pairs={{0,12},{1,13},{2,14},{3,15},{4,0},{5,1},{6,2},{7,3},{8,4},{9,5},{1... | collective-permute-start | bytes 1179656 | tf_op jit(solution)/shard_map/ppermute | solution.py:11
  187.4 14.3 %collective-permute-start.4 = (bf16[256,768]{1,0:T(8,128)(2,1)S(1)}, bf16[256,768]{1,0:T(8,128)(2,1)S(1)}, u32[]{:S(2)}, u32[]{:S(2)}) collective-permute-start(bf16[256,768]{1,0:T(8,128)(2,1)S(1)} %get-tuple-element.5), channel_id=1, source_target_pairs={{0,1},{1,2},{2,3},{3,4},{4,5},{5,6},{6,7},{7,8},{8,9},{9,10},{10,1... | collective-permute-start | bytes 1179656 | tf_op jit(solution)/shard_map/ppermute | solution.py:11
  187.5 14.2 %collective-permute-start.6 = (bf16[256,768]{1,0:T(8,128)(2,1)S(1)}, bf16[256,768]{1,0:T(8,128)(2,1)S(1)}, u32[]{:S(2)}, u32[]{:S(2)}) collective-permute-start(bf16[256,768]{1,0:T(8,128)(2,1)S(1)} %get-tuple-element.6), channel_id=1, source_target_pairs={{0,4},{1,5},{2,6},{3,7},{4,8},{5,9},{6,10},{7,11},{8,12},{9,13},{1... | collective-permute-start | bytes 1179656 | tf_op jit(solution)/shard_map/ppermute | solution.py:11
  188.1 17.8 %collective-permute-start.5 = (bf16[256,768]{1,0:T(8,128)(2,1)S(1)}, bf16[256,768]{1,0:T(8,128)(2,1)S(1)}, u32[]{:S(2)}, u32[]{:S(2)}) collective-permute-start(bf16[256,768]{1,0:T(8,128)(2,1)S(1)} %get-tuple-element.7), channel_id=1, source_target_pairs={{0,15},{1,0},{2,1},{3,2},{4,3},{5,4},{6,5},{7,6},{8,7},{9,8},{10,9... | collective-permute-start | bytes 1179656 | tf_op jit(solution)/shard_map/ppermute | solution.py:11
  192.2 20.2 %collective-permute-start.7 = (bf16[256,768]{1,0:T(8,128)(2,1)S(1)}, bf16[256,768]{1,0:T(8,128)(2,1)S(1)}, u32[]{:S(2)}, u32[]{:S(2)}) collective-permute-start(bf16[256,768]{1,0:T(8,128)(2,1)S(1)} %get-tuple-element.8), channel_id=1, source_target_pairs={{0,12},{1,13},{2,14},{3,15},{4,0},{5,1},{6,2},{7,3},{8,4},{9,5},{1... | collective-permute-start | bytes 1179656 | tf_op jit(solution)/shard_map/ppermute | solution.py:11
where the time goes:
time: 233 us; the launch traced here: 232 us
  other arithmetic  80.6 us (35%)
  waiting for transfers between devices  68 us (29%)
  local copies, waits for them, and re-layouts  45.4 us (19%)
  matrix products  20.3 us (9%)
  starting transfers between devices  17.7 us (8%)
    ppermute x8, waiting for transfers between devices, passed_along(): lax.ppermute(value, axis, [(i, (i + by) % count) for i in range(count)])  38.8 us
    scatter-add x2, other arithmetic, operate(): summed = empty.at[nodes.reshape(-1)].add(products.reshape(-1, width))  33.9 us
    all_to_all x1, waiting for transfers between devices, local(): lax.all_to_all(rotated_rows, 'band', split_axis=1, concat_axis=0, tiled=T...  29.2 us
    scatter-add x2, other arithmetic, operate(): return summed.at[flat_faces].add(incoming)  24.8 us
    gather x2, local copies, waits for them, and re-layouts, operate(): picked = vectors[nodes]  24.2 us
    gather x2, local copies, waits for them, and re-layouts, operate(): blocks = rounded[flat_faces].reshape(4, -1, width)  15.1 us
    dot_general x2, matrix products, operate(): jnp.einsum('cij,cjb->cib', cell_ham, picked, preferred_element_type=jnp.f...  13.9 us
    ppermute x8, starting transfers between devices, passed_along(): lax.ppermute(value, axis, [(i, (i + by) % count) for i in range(count)])  12.7 us
  transfers between devices with their start and end apart: 9, of which 7 were waited for; matrix products, arithmetic and copies ran while one was open for 0% of the time, Pallas kernels for 0%

commit v1 on v0

v1 whole, which is shorter than its diff:
```python
import functools
import math

import jax
import jax.numpy as jnp
from jax import lax
from jax.experimental import pallas as pl
from jax.experimental.pallas import tpu as pltpu
from jax.sharding import PartitionSpec as P

GRID_W = 4
MESH = pl.DeviceIdType.MESH
BF16 = jnp.bfloat16
F32 = jnp.float32


def dot(a, b):
    return jnp.dot(a, b, preferred_element_type=F32)


def hot(condition):
    return jnp.where(condition, 1.0, 0.0).astype(BF16)


def kernel(bands, parts, psi, ritz, ham, cell_row, cell_col, node_row, node_col, out,
           turned, arrived, rotated, onehot, products, dense, summed, first, leaving, landing,
           row_send, row_recv, face_send, face_recv):
    me_b = lax.axis_index("band")
    me_p = lax.axis_index("mesh")
    chunks, nloc, width = arrived.shape
    rows = psi.shape[0]
    group = ritz.shape[1] // bands
    shared = landing.shape[3]
    face_rows = 4 * shared
    cells, size = ham.shape[0], ham.shape[1]
    tile = math.gcd(face_rows, nloc)

    routes = ((3, 2, GRID_W), (2, 3, -GRID_W), (1, 0, 1), (0, 1, -1))

    def part(offset):
        return lax.rem(me_p + offset + parts, parts)

    def partner(offset):
        return lax.rem(me_b + offset, bands)

    barrier = pltpu.get_barrier_semaphore()
    for offset in range(1, bands):
        pl.semaphore_signal(barrier, inc=1, device_id=(partner(offset), me_p), device_id_type=MESH)
    for _, _, offset in routes:
        pl.semaphore_signal(barrier, inc=1, device_id=(me_b, part(offset)), device_id_type=MESH)
    pl.semaphore_wait(barrier, bands + 3)

    def own_rows(k, owner):
        return arrived.at[k, pl.ds(pl.multiple_of(owner * rows, rows), rows), :]

    def row_copy(k, offset):
        return pltpu.make_async_remote_copy(
            src_ref=turned.at[offset - 1, k],
            dst_ref=own_rows(k, me_b),
            send_sem=row_send.at[offset - 1, k],
            recv_sem=row_recv.at[offset - 1, k],
            device_id=(partner(offset), me_p),
            device_id_type=MESH,
        )

    def ritz_columns(owner, k):
        return ritz[:, pl.ds(pl.multiple_of(owner * group + k * width, 128), width)]

    for offset in range(1, bands):
        @pl.loop(0, chunks)
        def _(k):
            turned[offset - 1, k] = dot(psi[...], ritz_columns(partner(offset), k)).astype(BF16)
            row_copy(k, offset).start()

    @pl.loop(0, chunks)
    def _(k):
        own_rows(k, me_b)[...] = dot(psi[...], ritz_columns(me_b, k)).astype(BF16)

    total = cells * size
    step = 256

    @pl.loop(0, nloc // step)
    def _(r):
        at = pl.multiple_of(r * step, step)
        numbers = lax.broadcasted_iota(jnp.int32, (step, total), 0) + at
        onehot[pl.ds(at, step), :] = hot(numbers == cell_row[...])

    @pl.loop(0, nloc // step)
    def _(c):
        at = pl.multiple_of(c * step, step)
        for cell in range(cells):
            numbers = lax.broadcasted_iota(jnp.int32, (size, step), 1) + at
            picked = hot(numbers == cell_col[cell * size:(cell + 1) * size, :])
            products[cell * size:(cell + 1) * size, :] = dot(ham[cell], picked).astype(BF16)
        for r in range(0, nloc, tile):
            dense[r:r + tile, pl.ds(at, step)] = dot(onehot[r:r + tile, :], products[...]).astype(BF16)

    @pl.loop(0, nloc // step)
    def _(r):
        at = pl.multiple_of(r * step, step)
        numbers = lax.broadcasted_iota(jnp.int32, (step, nloc), 0) + at
        onehot[pl.ds(at, step), :nloc] = hot(numbers == node_row[...])

    def face_copy(turn, k, route):
        block, slot, offset = route
        return pltpu.make_async_remote_copy(
            src_ref=leaving.at[turn, k, block],
            dst_ref=landing.at[turn, k, slot],
            send_sem=face_send.at[turn, k, slot],
            recv_sem=face_recv.at[turn, k, slot],
            device_id=(me_b, part(offset)),
            device_id_type=MESH,
        )

    def operate(turn, k, vectors):
        for half in (1, 0):
            for at in range(half * 2 * shared, (half + 1) * 2 * shared, tile):
                part_sum = dot(dense[at:at + tile, :], vectors[k])
                summed[k, at:at + tile, :] = part_sum
                rounded = part_sum.astype(BF16)
                for block in range(at // shared, max(at // shared + 1, (at + tile) // shared)):
                    low = max(at, block * shared)
                    high = min(at + tile, (block + 1) * shared)
                    leaving[turn, k, block, low - block * shared:high - block * shared, :] = rounded[low - at:high - at]
            for route in routes:
                if route[0] // 2 == half:
                    face_copy(turn, k, route).start()
        for at in range(face_rows, nloc, tile):
            summed[k, at:at + tile, :] = dot(dense[at:at + tile, :], vectors[k])

    @pl.loop(0, chunks)
    def _(k):
        for offset in range(1, bands):
            row_copy(k, offset).wait()
        for r in range(0, nloc, tile):
            rotated[k, r:r + tile, :] = dot(onehot[r:r + tile, :nloc], arrived[k]).astype(BF16)
        operate(0, k, rotated)

    def assembled(turn, k):
        for route in routes:
            face_copy(turn, k, route).wait()
        for slot in range(4):
            at = slice(slot * shared, (slot + 1) * shared)
            summed[k, at, :] = summed[k, at, :] + landing[turn, k, slot].astype(F32)

    @pl.loop(0, chunks)
    def _(k):
        assembled(0, k)
        first[k] = ((summed[k] - 0.25 * rotated[k].astype(F32)) / 2.0).astype(BF16)
        operate(1, k, first)

    @pl.loop(0, nloc // step)
    def _(r):
        at = pl.multiple_of(r * step, step)
        numbers = lax.broadcasted_iota(jnp.int32, (step, nloc), 1)
        onehot[pl.ds(at, step), :nloc] = hot(numbers == node_col[pl.ds(at, step), :])

    @pl.loop(0, chunks)
    def _(k):
        assembled(1, k)
        value = 2.0 * (summed[k] - 0.25 * first[k].astype(F32)) / 2.0 - rotated[k].astype(F32)
        arrived[k] = value.astype(BF16)
        columns = pl.ds(pl.multiple_of(k * width, 128), width)
        for r in range(0, nloc, tile):
            out[r:r + tile, columns] = dot(onehot[r:r + tile, :nloc], arrived[k]).astype(BF16)


def local(bands, parts, psi, ritz, cell_ham, cell_nodes, face_nodes):
    rows = psi.shape[1]
    nloc = rows * bands
    group = ritz.shape[1] // bands
    cells, size = cell_ham.shape[1], cell_ham.shape[2]
    shared = face_nodes.shape[2]
    faces = face_nodes.reshape(-1)
    numbers = jnp.arange(nloc, dtype=jnp.int32)
    match = faces[:, None] == numbers[None, :]
    order = jnp.arange(1, faces.shape[0] + 1, dtype=jnp.int32)
    face_at = jnp.sum(jnp.where(match, order[:, None], 0), axis=0)
    inner = face_at == 0
    before = jnp.sum(jnp.where((numbers[:, None] < numbers[None, :]) & inner[:, None], 1, 0), axis=0)
    place = jnp.where(inner, faces.shape[0] + before, face_at - 1).astype(jnp.int32)
    nodes = cell_nodes.reshape(-1)
    cell_place = jnp.sum(jnp.where(nodes[:, None] == numbers[None, :], place[None, :], 0), axis=1).astype(jnp.int32)

    width = 256 if group % 256 == 0 else 128
    chunks = group // width
    vmem = pl.BlockSpec(memory_space=pltpu.VMEM)
    out = pl.pallas_call(
        functools.partial(kernel, bands, parts),
        out_shape=jax.ShapeDtypeStruct((nloc, group), BF16),
        in_specs=[vmem] * 7,
        out_specs=vmem,
        scratch_shapes=[
            pltpu.VMEM((bands - 1, chunks, rows, width), BF16),
            pltpu.VMEM((chunks, nloc, width), BF16),
            pltpu.VMEM((chunks, nloc, width), BF16),
            pltpu.VMEM((nloc, max(cells * size, nloc)), BF16),
            pltpu.VMEM((cells * size, 256), BF16),
            pltpu.VMEM((nloc, nloc), BF16),
            pltpu.VMEM((chunks, nloc, width), F32),
            pltpu.VMEM((chunks, nloc, width), BF16),
            pltpu.VMEM((2, chunks, 4, shared, width), BF16),
            pltpu.VMEM((2, chunks, 4, shared, width), BF16),
            pltpu.SemaphoreType.DMA((bands - 1, chunks)),
            pltpu.SemaphoreType.DMA((bands - 1, chunks)),
            pltpu.SemaphoreType.DMA((2, chunks, 4)),
            pltpu.SemaphoreType.DMA((2, chunks, 4)),
        ],
        compiler_params=pltpu.CompilerParams(
            collective_id=0, has_side_effects=True, vmem_limit_bytes=62 * 1024 * 1024
        ),
    )(psi[0], ritz, cell_ham[0], cell_place[None, :], cell_place[:, None], place[None, :], place[:, None])
    return out[None]


def solution(mesh):
    return jax.shard_map(
        functools.partial(local, mesh.shape["band"], mesh.shape["mesh"]),
        mesh=mesh,
        in_specs=(
            P("mesh", "band", None),
            P(),
            P("mesh", None, None, None),
            P("mesh", None, None),
            P("mesh", None, None),
        ),
        out_specs=P("mesh", None, "band"),
        check_vma=False,
    )
```

time: 233 us -> 96 us (0.41)
  Pallas kernels: 0 us -> 83 us
  other arithmetic: 80.6 us -> 4.99 us
  waiting for transfers between devices: 68 us -> 0 us
  local copies, waits for them, and re-layouts: 45.4 us -> 7.71 us
  matrix products: 20.3 us -> 0 us
  starting transfers between devices: 17.7 us -> 0 us
    pallas_call x0 -> x1, Pallas kernels: none -> 83 us  [local(): pl.pallas_call(functools.partial(kernel, bands, parts), out_shape=jax.Sha...]
    scatter-add x4 -> x0, other arithmetic: 58.7 us -> none  [the longest x2 33.9 us: operate(): summed = empty.at[nodes.reshape(-1)].add(products.reshape(-1, width))]
    gather x4 -> x0, local copies, waits for them, and re-layouts: 39.2 us -> none  [the longest x2 24.2 us: operate(): picked = vectors[nodes]]
    ppermute x8 -> x0, waiting for transfers between devices: 38.8 us -> none  [passed_along(): lax.ppermute(value, axis, [(i, (i + by) % count) for i in range(count)])]
    all_to_all x1 -> x0, waiting for transfers between devices: 29.2 us -> none  [local(): lax.all_to_all(rotated_rows, 'band', split_axis=1, concat_axis=0, tiled=T...]
    dot_general x3 -> x0, matrix products: 20.3 us -> none  [the longest x2 13.9 us: operate(): jnp.einsum('cij,cjb->cib', cell_ham, picked, preferred_element_type=jnp.f...]
    convert_element_type x3 -> x0, other arithmetic: 13.2 us -> none  [the longest x2 7.96 us: operate(): rounded = summed.astype(jnp.bfloat16)]
    ppermute x8 -> x0, starting transfers between devices: 12.7 us -> none  [passed_along(): lax.ppermute(value, axis, [(i, (i + by) % count) for i in range(count)])]
  transfers between devices with their start and end apart: 9 -> 0, of which waited for: 7 -> 0; matrix products, arithmetic and copies ran while one was open for 0% -> 0% of each run, Pallas kernels for 0% -> 0%
where the time goes in v1:
time: 96 us; the launch traced here: 95.8 us
  Pallas kernels  83 us (86%)
  local copies, waits for them, and re-layouts  7.71 us (8%)
  other arithmetic  4.99 us (5%)
    pallas_call x1, Pallas kernels, local(): pl.pallas_call(functools.partial(kernel, bands, parts), out_shape=jax.Sha...  83 us
    unnamed x5, local copies, waits for them, and re-layouts  4.61 us
    reduce_sum x1, other arithmetic, local(): jnp.sum(jnp.where((numbers[:, None] < numbers[None, :]) & inner[:, None],...  2.29 us

profile of v1, /device:TPU:0, one launch (start us, length us, event | category | flops | bytes accessed | tf_op | source)
XLA Modules:
  0.0 95.8 jit_solution(3866616935164848034)
XLA Ops:
  0.0 0.7 copy.11
  0.7 0.8 select_reduce_fusion.2
  1.5 2.3 %select_reduce_fusion.1 = s32[1536]{0:T(1024)S(1)} fusion(pred[1536]{0:T(1024)(128)(4,1)S(1)} %broadcast_compare_fusion), kind=kLoop, calls=%fused_computation.2 | loop fusion | flops 9435648 | bytes 7680 | tf_op jit(solution)/shard_map/reduce_sum | solution.py:180
  3.8 0.6 select_n.41.node_row
  4.4 0.7 copy.10
  5.1 1.9 %select_reduce_fusion = s32[2048]{0:T(1024)S(1)} fusion(s32[1536]{0:T(1024)S(1)} %add_select_fusion, s32[2048]{0:T(1024)S(1)} %bitcast.15), kind=kLoop, calls=%fused_computation | loop fusion | flops 9435136 | bytes 22528 | tf_op jit(solution)/shard_map/reduce_sum | solution.py:183
  7.0 0.0 copy-start
  7.0 1.2 %select_n.43.node_col = s32[1536,1]{1,0:T(8,128)} reshape(s32[1536]{0:T(1024)S(1)} %add_select_fusion) | data formatting | bytes 12288 | tf_op jit(solution)/shard_map/jit(_where)/select_n | solution.py:181
  8.2 1.3 %copy.8.cell_col = s32[2048,1]{1,0:T(8,128)} copy(s32[2048,1]{0,1:T(1,128)S(1)} %bitcast.12) | data formatting | bytes 16384 | tf_op jit(solution)/shard_map/broadcast_in_dim | solution.py:212
  9.5 0.0 copy-done
  9.5 83.0 %shard_map.55 = bf16[1536,768]{1,0:T(8,128)(2,1)} custom-call(bf16[768,1536]{1,0:T(8,128)(2,1)} %bitcast.10, bf16[1536,1536]{1,0:T(8,128)(2,1)} %ritz.1, bf16[4,512,512]{2,1,0:T(8,128)(2,1)} %bitcast.11, s32[1,2048]{1,0:T(1,128)} %bitcast.13, s32[2048,1]{1,0:T(8,128)} %copy.8.cell_col, s32[1,1536]{1,0:T(1,128)} %select_n.41.node_row, ...), custom_call_target="tpu_custom_call" | custom-call | tf_op jit(solution)/shard_map/pallas_call | solution.py:188
  92.5 3.2 %copy.13 = bf16[1,1536,768]{2,1,0:T(8,128)(2,1)} copy(bf16[1,1536,768]{2,1,0:T(8,128)(2,1)} %bitcast.9) | data formatting | bytes 4718592
  (3 shorter events, 0.0 us)
Async XLA Ops:
  7.0 2.5 %copy-start = (s32[2048]{0:T(1024)}, s32[2048]{0:T(1024)S(1)}, u32[]{:S(2)}) copy-start(s32[2048]{0:T(1024)S(1)} %select_reduce_fusion) | copy-start | bytes 24580

commit v2 on v1

v2 whole, which is shorter than its diff:
```python
import functools
import math

import jax
import jax.numpy as jnp
from jax import lax
from jax.experimental import pallas as pl
from jax.experimental.pallas import tpu as pltpu
from jax.sharding import PartitionSpec as P

GRID_W = 4
MESH = pl.DeviceIdType.MESH
BF16 = jnp.bfloat16
F32 = jnp.float32


def dot(a, b):
    return jnp.dot(a, b, preferred_element_type=F32)


def hot(condition):
    return jnp.where(condition, 1.0, 0.0).astype(BF16)


def upright(row):
    return jnp.broadcast_to(row, (128, row.shape[1])).T


def across(column, width):
    return jnp.concatenate([column] * (width // 128), axis=1)


def kernel(bands, parts, psi_hbm, ritz_hbm, ham_hbm, cell_nodes, face_nodes, out,
           psi, ritz, ham, turned, arrived, rotated, cell_hot, node_hot, picked, dense, summed, first, leaving, landing,
           columns, finished, load, store, row_send, row_recv, face_send, face_recv):
    me_b = lax.axis_index("band")
    me_p = lax.axis_index("mesh")
    chunks, nloc, width = arrived.shape
    rows = psi.shape[0]
    group = ritz.shape[2]
    shared = landing.shape[3]
    face_rows = 4 * shared
    cells, size = ham.shape[0], ham.shape[1]
    total = cells * size
    tile = math.gcd(2 * shared, nloc)
    step = 256

    routes = ((3, 2, GRID_W), (2, 3, -GRID_W), (1, 0, 1), (0, 1, -1))

    def part(offset):
        return lax.rem(me_p + offset + parts, parts)

    def partner(offset):
        return lax.rem(me_b + offset, bands)

    def ritz_load(offset):
        at = pl.multiple_of(partner(offset) * group, 128)
        return pltpu.make_async_copy(ritz_hbm.at[:, pl.ds(at, group)], ritz.at[offset], load.at[2 + offset])

    psi_load = pltpu.make_async_copy(psi_hbm, psi, load.at[0])
    ham_load = pltpu.make_async_copy(ham_hbm, ham, load.at[1])
    psi_load.start()
    for offset in range(1, bands):
        ritz_load(offset).start()
    ritz_load(0).start()
    ham_load.start()

    barrier = pltpu.get_barrier_semaphore()
    for offset in range(1, bands):
        pl.semaphore_signal(barrier, inc=1, device_id=(partner(offset), me_p), device_id_type=MESH)
    for _, _, offset in routes:
        pl.semaphore_signal(barrier, inc=1, device_id=(me_b, part(offset)), device_id_type=MESH)
    pl.semaphore_wait(barrier, bands + 3)

    def own_rows(k, owner):
        return arrived.at[k, pl.ds(pl.multiple_of(owner * rows, rows), rows), :]

    def row_copy(k, offset):
        return pltpu.make_async_remote_copy(
            src_ref=turned.at[offset - 1, k],
            dst_ref=own_rows(k, me_b),
            send_sem=row_send.at[offset - 1, k],
            recv_sem=row_recv.at[offset - 1, k],
            device_id=(partner(offset), me_p),
            device_id_type=MESH,
        )

    def chunk(k):
        return pl.ds(pl.multiple_of(k * width, 128), width)

    psi_load.wait()
    for offset in range(1, bands):
        ritz_load(offset).wait()

    @pl.loop(0, chunks)
    def _(k):
        for offset in range(1, bands):
            turned[offset - 1, k] = dot(psi[...], ritz[offset, :, chunk(k)]).astype(BF16)
            row_copy(k, offset).start()

    for face in range(4):
        columns[face * shared:(face + 1) * shared, :] = upright(face_nodes[face:face + 1, :])
    lanes = lax.broadcasted_iota(jnp.int32, (1, nloc), 1)

    def find_face(block, found):
        at = pl.multiple_of(block * step, step)
        order = lax.broadcasted_iota(jnp.int32, (step, nloc), 0) + (at + 1)
        numbers = lax.broadcasted_iota(jnp.int32, (step, nloc), 1)
        match = across(columns[pl.ds(at, step), :], nloc) == numbers
        return found + jnp.sum(jnp.where(match, order, 0), axis=0, keepdims=True)

    found = lax.fori_loop(0, face_rows // step, find_face, jnp.zeros((1, nloc), jnp.int32))
    inner = jnp.where(found == 0, 1, 0)
    before = jnp.broadcast_to(inner, (8, nloc))
    eight = lax.broadcasted_iota(jnp.int32, (8, nloc), 1)
    shift = 1
    while shift < nloc:
        before = before + jnp.where(eight >= shift, pltpu.roll(before, shift, 1), 0)
        shift *= 2
    place = jnp.where(found == 0, before[:1, :] + (face_rows - 1), found - 1)

    @pl.loop(0, nloc // step)
    def _(r):
        at = pl.multiple_of(r * step, step)
        numbers = lax.broadcasted_iota(jnp.int32, (step, nloc), 0) + at
        node_hot[pl.ds(at, step), :] = hot(numbers == place)

    columns[:nloc, :] = upright(place)
    listed = jnp.concatenate([cell_nodes[cell:cell + 1, :] for cell in range(cells)], axis=1)

    def find_place(block, places):
        at = pl.multiple_of(block * step, step)
        numbers = lax.broadcasted_iota(jnp.int32, (step, total), 0) + at
        values = across(columns[pl.ds(at, step), :], total)
        return places + jnp.sum(jnp.where(numbers == listed, values, 0), axis=0, keepdims=True)

    cell_place = lax.fori_loop(0, nloc // step, find_place, jnp.zeros((1, total), jnp.int32))
    columns[nloc:, :] = upright(cell_place)

    @pl.loop(0, total // step)
    def _(r):
        at = pl.multiple_of(r * step, step)
        numbers = lax.broadcasted_iota(jnp.int32, (step, nloc), 1)
        cell_hot[pl.ds(at, step), :nloc] = hot(numbers == across(columns[pl.ds(nloc + at, step), :], nloc))

    ritz_load(0).wait()

    @pl.loop(0, chunks)
    def _(k):
        own_rows(k, me_b)[...] = dot(psi[...], ritz[0, :, chunk(k)]).astype(BF16)

    ham_load.wait()

    def build(low, high):
        for at in range(low, high, tile):
            numbers = lax.broadcasted_iota(jnp.int32, (tile, size), 0) + at
            for cell in range(cells):
                span = slice(cell * size, (cell + 1) * size)
                picked[:, span] = dot(hot(numbers == cell_place[:, span]), ham[cell]).astype(BF16)

            @pl.loop(0, nloc // step)
            def _(c):
                to = pl.multiple_of(c * step, step)
                dense[at:at + tile, pl.ds(to, step)] = dot(picked[...], cell_hot[:, pl.ds(to, step)]).astype(BF16)

    def face_copy(turn, k, route):
        block, slot, offset = route
        return pltpu.make_async_remote_copy(
            src_ref=leaving.at[turn, k, block],
            dst_ref=landing.at[turn, k, slot],
            send_sem=face_send.at[turn, k, slot],
            recv_sem=face_recv.at[turn, k, slot],
            device_id=(me_b, part(offset)),
            device_id_type=MESH,
        )

    def operate_faces(turn, k, vectors, half):
        for at in range(half * 2 * shared, (half + 1) * 2 * shared, tile):
            part_sum = dot(dense[at:at + tile, :], vectors[k])
            summed[k, at:at + tile, :] = part_sum
            rounded = part_sum.astype(BF16)
            for block in range(4):
                low = max(at, block * shared)
                high = min(at + tile, (block + 1) * shared)
                if low < high:
                    leaving[turn, k, block, low - block * shared:high - block * shared, :] = rounded[low - at:high - at]
        for route in routes:
            if route[0] // 2 == half:
                face_copy(turn, k, route).start()

    def operate_inner(k, vectors):
        for at in range(face_rows, nloc, tile):
            summed[k, at:at + tile, :] = dot(dense[at:at + tile, :], vectors[k])

    def receive(k):
        for offset in range(1, bands):
            row_copy(k, offset).wait()

        @pl.loop(0, nloc // tile)
        def _(r):
            at = pl.ds(pl.multiple_of(r * tile, tile), tile)
            rotated[k, at, :] = dot(node_hot[at, :], arrived[k]).astype(BF16)

    build(2 * shared, face_rows)
    receive(0)
    operate_faces(0, 0, rotated, 1)
    build(0, 2 * shared)
    operate_faces(0, 0, rotated, 0)

    @pl.loop(1, chunks)
    def _(k):
        receive(k)
        operate_faces(0, k, rotated, 1)
        operate_faces(0, k, rotated, 0)

    build(face_rows, nloc)

    def assembled(turn, k):
        for route in routes:
            face_copy(turn, k, route).wait()
        for slot in range(4):
            at = slice(slot * shared, (slot + 1) * shared)
            summed[k, at, :] = summed[k, at, :] + landing[turn, k, slot].astype(F32)

    @pl.loop(0, chunks)
    def _(k):
        operate_inner(k, rotated)
        assembled(0, k)
        first[k] = ((summed[k] - 0.25 * rotated[k].astype(F32)) / 2.0).astype(BF16)
        operate_faces(1, k, first, 1)
        operate_faces(1, k, first, 0)
        operate_inner(k, first)

    @pl.loop(0, nloc // step)
    def _(r):
        at = pl.multiple_of(r * step, step)
        numbers = lax.broadcasted_iota(jnp.int32, (step, nloc), 1)
        node_hot[pl.ds(at, step), :] = hot(numbers == across(columns[pl.ds(at, step), :], nloc))

    def put(k):
        return pltpu.make_async_copy(finished.at[k], out.at[:, chunk(k)], store.at[k])

    @pl.loop(0, chunks)
    def _(k):
        assembled(1, k)
        value = 2.0 * (summed[k] - 0.25 * first[k].astype(F32)) / 2.0 - rotated[k].astype(F32)
        arrived[k] = value.astype(BF16)

        @pl.loop(0, nloc // tile)
        def _(r):
            at = pl.ds(pl.multiple_of(r * tile, tile), tile)
            finished[k, at, :] = dot(node_hot[at, :], arrived[k]).astype(BF16)

        put(k).start()

    @pl.loop(0, chunks)
    def _(k):
        put(k).wait()


def local(bands, parts, psi, ritz, cell_ham, cell_nodes, face_nodes):
    rows = psi.shape[1]
    nloc = rows * bands
    group = ritz.shape[1] // bands
    cells, size = cell_ham.shape[1], cell_ham.shape[2]
    shared = face_nodes.shape[2]
    width = 256 if group % 256 == 0 else 128
    chunks = group // width
    tile = math.gcd(2 * shared, nloc)
    anywhere = pl.BlockSpec(memory_space=pl.ANY)
    vmem = pl.BlockSpec(memory_space=pltpu.VMEM)
    out = pl.pallas_call(
        functools.partial(kernel, bands, parts),
        out_shape=jax.ShapeDtypeStruct((nloc, group), BF16),
        in_specs=[anywhere] * 3 + [vmem] * 2,
        out_specs=anywhere,
        scratch_shapes=[
            pltpu.VMEM((rows, ritz.shape[0]), BF16),
            pltpu.VMEM((bands, ritz.shape[0], group), BF16),
            pltpu.VMEM((cells, size, size), BF16),
            pltpu.VMEM((bands - 1, chunks, rows, width), BF16),
            pltpu.VMEM((chunks, nloc, width), BF16),
            pltpu.VMEM((chunks, nloc, width), BF16),
            pltpu.VMEM((cells * size, nloc), BF16),
            pltpu.VMEM((nloc, nloc), BF16),
            pltpu.VMEM((tile, cells * size), BF16),
            pltpu.VMEM((nloc, nloc), BF16),
            pltpu.VMEM((chunks, nloc, width), F32),
            pltpu.VMEM((chunks, nloc, width), BF16),
            pltpu.VMEM((2, chunks, 4, shared, width), BF16),
            pltpu.VMEM((2, chunks, 4, shared, width), BF16),
            pltpu.VMEM((nloc + cells * size, 128), jnp.int32),
            pltpu.VMEM((chunks, nloc, width), BF16),
            pltpu.SemaphoreType.DMA((2 + bands,)),
            pltpu.SemaphoreType.DMA((chunks,)),
            pltpu.SemaphoreType.DMA((bands - 1, chunks)),
            pltpu.SemaphoreType.DMA((bands - 1, chunks)),
            pltpu.SemaphoreType.DMA((2, chunks, 4)),
            pltpu.SemaphoreType.DMA((2, chunks, 4)),
        ],
        compiler_params=pltpu.CompilerParams(
            collective_id=0, has_side_effects=True, vmem_limit_bytes=62 * 1024 * 1024
        ),
    )(psi[0], ritz, cell_ham[0], cell_nodes[0], face_nodes[0])
    return out[None]


def solution(mesh):
    return jax.shard_map(
        functools.partial(local, mesh.shape["band"], mesh.shape["mesh"]),
        mesh=mesh,
        in_specs=(
            P("mesh", "band", None),
            P(),
            P("mesh", None, None, None),
            P("mesh", None, None),
            P("mesh", None, None),
        ),
        out_specs=P("mesh", None, "band"),
        check_vma=False,
    )
```

time: 96 us -> 80.6 us (0.84)
  Pallas kernels: 83 us -> 77.2 us
  other arithmetic: 4.99 us -> 0 us
  local copies, waits for them, and re-layouts: 7.71 us -> 3.22 us
    pallas_call x1, Pallas kernels: 83 us -> 77.2 us  [local(): pl.pallas_call(functools.partial(kernel, bands, parts), out_shape=jax.Sha...]
    reduce_sum x3 -> x0, other arithmetic: 4.97 us -> none  [the longest x1 2.29 us: local(): jnp.sum(jnp.where((numbers[:, None] < numbers[None, :]) & inner[:, None],...]
    select_n x2 -> x0, local copies, waits for them, and re-layouts: 1.75 us -> none  [local(): jnp.where(inner, faces.shape[0] + before, face_at - 1).astype(jnp.int32)]
    unnamed x5 -> x1, local copies, waits for them, and re-layouts: 4.61 us -> 3.22 us
    broadcast_in_dim x1 -> x0, local copies, waits for them, and re-layouts: 1.34 us -> none  [local(): cell_place[:, None]]
where the time goes in v2:
time: 80.6 us; the launch traced here: 80.4 us
  Pallas kernels  77.2 us (96%)
  local copies, waits for them, and re-layouts  3.22 us (4%)
    pallas_call x1, Pallas kernels, local(): pl.pallas_call(functools.partial(kernel, bands, parts), out_shape=jax.Sha...  77.2 us
    unnamed x1, local copies, waits for them, and re-layouts  3.22 us

profile of v2, /device:TPU:0, one launch (start us, length us, event | category | flops | bytes accessed | tf_op | source)
XLA Modules:
  0.0 80.4 jit_solution(17357742626254273047)
XLA Ops:
  0.0 77.2 %shard_map.55 = bf16[1536,768]{1,0:T(8,128)(2,1)} custom-call(bf16[768,1536]{1,0:T(8,128)(2,1)} %bitcast.6, bf16[1536,1536]{1,0:T(8,128)(2,1)} %ritz_hbm.1, bf16[4,512,512]{2,1,0:T(8,128)(2,1)} %bitcast.7, s32[4,512]{1,0:T(4,128)} %bitcast.8, s32[4,256]{1,0:T(4,128)} %bitcast.9), custom_call_target="tpu_custom_call" | custom-call | tf_op jit(solution)/shard_map/pallas_call | solution.py:272
  77.2 3.2 %copy.7 = bf16[1,1536,768]{2,1,0:T(8,128)(2,1)} copy(bf16[1,1536,768]{2,1,0:T(8,128)(2,1)} %bitcast.5) | data formatting | bytes 4718592

commit v3 on v2

--- a/solution.py
+++ b/solution.py
@@ -70,7 +70,6 @@
         pl.semaphore_signal(barrier, inc=1, device_id=(partner(offset), me_p), device_id_type=MESH)
     for _, _, offset in routes:
         pl.semaphore_signal(barrier, inc=1, device_id=(me_b, part(offset)), device_id_type=MESH)
-    pl.semaphore_wait(barrier, bands + 3)
 
     def own_rows(k, owner):
         return arrived.at[k, pl.ds(pl.multiple_of(owner * rows, rows), rows), :]
@@ -88,16 +87,6 @@
     def chunk(k):
         return pl.ds(pl.multiple_of(k * width, 128), width)
 
-    psi_load.wait()
-    for offset in range(1, bands):
-        ritz_load(offset).wait()
-
-    @pl.loop(0, chunks)
-    def _(k):
-        for offset in range(1, bands):
-            turned[offset - 1, k] = dot(psi[...], ritz[offset, :, chunk(k)]).astype(BF16)
-            row_copy(k, offset).start()
-
     for face in range(4):
         columns[face * shared:(face + 1) * shared, :] = upright(face_nodes[face:face + 1, :])
     lanes = lax.broadcasted_iota(jnp.int32, (1, nloc), 1)
@@ -143,12 +132,21 @@
         numbers = lax.broadcasted_iota(jnp.int32, (step, nloc), 1)
         cell_hot[pl.ds(at, step), :nloc] = hot(numbers == across(columns[pl.ds(nloc + at, step), :], nloc))
 
+    def turn(k):
+        for offset in range(1, bands):
+            turned[offset - 1, k] = dot(psi[...], ritz[offset, :, chunk(k)]).astype(BF16)
+            row_copy(k, offset).start()
+
+    def keep(k):
+        own_rows(k, me_b)[...] = dot(psi[...], ritz[0, :, chunk(k)]).astype(BF16)
+
+    psi_load.wait()
+    for offset in range(1, bands):
+        ritz_load(offset).wait()
+    pl.semaphore_wait(barrier, bands + 3)
+    turn(0)
     ritz_load(0).wait()
-
-    @pl.loop(0, chunks)
-    def _(k):
-        own_rows(k, me_b)[...] = dot(psi[...], ritz[0, :, chunk(k)]).astype(BF16)
-
+    keep(0)
     ham_load.wait()
 
     def build(low, high):
@@ -184,9 +182,15 @@
                 high = min(at + tile, (block + 1) * shared)
                 if low < high:
                     leaving[turn, k, block, low - block * shared:high - block * shared, :] = rounded[low - at:high - at]
-        for route in routes:
-            if route[0] // 2 == half:
-                face_copy(turn, k, route).start()
+        for late in (False, True):
+            for route in routes:
+                if route[0] // 2 == half:
+                    target = me_p + route[2]
+                    wraps = jnp.logical_or(target < 0, target >= parts)
+
+                    @pl.when(wraps if late else jnp.logical_not(wraps))
+                    def _(route=route):
+                        face_copy(turn, k, route).start()
 
     def operate_inner(k, vectors):
         for at in range(face_rows, nloc, tile):
@@ -200,20 +204,6 @@
         def _(r):
             at = pl.ds(pl.multiple_of(r * tile, tile), tile)
             rotated[k, at, :] = dot(node_hot[at, :], arrived[k]).astype(BF16)
-
-    build(2 * shared, face_rows)
-    receive(0)
-    operate_faces(0, 0, rotated, 1)
-    build(0, 2 * shared)
-    operate_faces(0, 0, rotated, 0)
-
-    @pl.loop(1, chunks)
-    def _(k):
-        receive(k)
-        operate_faces(0, k, rotated, 1)
-        operate_faces(0, k, rotated, 0)
-
-    build(face_rows, nloc)
 
     def assembled(turn, k):
         for route in routes:
@@ -222,14 +212,43 @@
             at = slice(slot * shared, (slot + 1) * shared)
             summed[k, at, :] = summed[k, at, :] + landing[turn, k, slot].astype(F32)
 
-    @pl.loop(0, chunks)
-    def _(k):
+    def advance(k):
         operate_inner(k, rotated)
         assembled(0, k)
         first[k] = ((summed[k] - 0.25 * rotated[k].astype(F32)) / 2.0).astype(BF16)
         operate_faces(1, k, first, 1)
         operate_faces(1, k, first, 0)
-        operate_inner(k, first)
+
+    build(2 * shared, face_rows)
+
+    @pl.loop(1, chunks)
+    def _(k):
+        turn(k)
+
+    @pl.loop(1, chunks)
+    def _(k):
+        keep(k)
+
+    receive(0)
+    operate_faces(0, 0, rotated, 1)
+    build(0, 2 * shared)
+    operate_faces(0, 0, rotated, 0)
+
+    @pl.loop(1, chunks)
+    def _(k):
+        receive(k)
+        operate_faces(0, k, rotated, 1)
+        operate_faces(0, k, rotated, 0)
+
+        @pl.when(k == 1)
+        def _():
+            build(face_rows, nloc)
+
+        advance(k - 1)
+
+    if chunks == 1:
+        build(face_rows, nloc)
+    advance(chunks - 1)
 
     @pl.loop(0, nloc // step)
     def _(r):
@@ -242,6 +261,7 @@
 
     @pl.loop(0, chunks)
     def _(k):
+        operate_inner(k, first)
         assembled(1, k)
         value = 2.0 * (summed[k] - 0.25 * first[k].astype(F32)) / 2.0 - rotated[k].astype(F32)
         arrived[k] = value.astype(BF16)
@@ -256,6 +276,24 @@
     @pl.loop(0, chunks)
     def _(k):
         put(k).wait()
+
+
+def copy_kernel(source, target, held, taken, given):
+    pieces, rows = held.shape[0], held.shape[1]
+
+    def take(i):
+        return pltpu.make_async_copy(source.at[i * rows:(i + 1) * rows, :], held.at[i], taken.at[i])
+
+    def give(i):
+        return pltpu.make_async_copy(held.at[i], target.at[i * rows:(i + 1) * rows, :], given.at[i])
+
+    for i in range(pieces):
+        take(i).start()
+    for i in range(pieces):
+        take(i).wait()
+        give(i).start()
+    for i in range(pieces):
+        give(i).wait()
 
 
 def local(bands, parts, psi, ritz, cell_ham, cell_nodes, face_nodes):
@@ -302,6 +340,18 @@
             collective_id=0, has_side_effects=True, vmem_limit_bytes=62 * 1024 * 1024
         ),
     )(psi[0], ritz, cell_ham[0], cell_nodes[0], face_nodes[0])
+    pieces = 6 if nloc % 48 == 0 else 1
+    out = pl.pallas_call(
+        copy_kernel,
+        out_shape=jax.ShapeDtypeStruct((nloc, group), BF16),
+        in_specs=[anywhere],
+        out_specs=anywhere,
+        scratch_shapes=[
+            pltpu.VMEM((pieces, nloc // pieces, group), BF16),
+            pltpu.SemaphoreType.DMA((pieces,)),
+            pltpu.SemaphoreType.DMA((pieces,)),
+        ],
+    )(out)
     return out[None]
 
 

time: 80.6 us -> 80.1 us (level)
  local copies, waits for them, and re-layouts: 3.22 us -> 0 us
  Pallas kernels: 77.2 us -> 79.7 us
    unnamed x1 -> x0, local copies, waits for them, and re-layouts: 3.22 us -> none
    pallas_call x0 -> x1, Pallas kernels: none -> 2.49 us  [local(): pl.pallas_call(copy_kernel, out_shape=jax.ShapeDtypeStruct((nloc, group),...]
where the time goes in v3:
time: 80.1 us; the launch traced here: 79.9 us
  Pallas kernels  79.7 us (100%)
    pallas_call x1, Pallas kernels, local(): pl.pallas_call(functools.partial(kernel, bands, parts), out_shape=jax.Sha...  77.2 us
    pallas_call x1, Pallas kernels, local(): pl.pallas_call(copy_kernel, out_shape=jax.ShapeDtypeStruct((nloc, group),...  2.49 us

profile of v3, /device:TPU:0, one launch (start us, length us, event | category | flops | bytes accessed | tf_op | source)
XLA Modules:
  0.0 79.9 jit_solution(10907055688086295297)
XLA Ops:
  0.0 77.2 %shard_map.55.source = bf16[1536,768]{1,0:T(8,128)(2,1)} custom-call(bf16[768,1536]{1,0:T(8,128)(2,1)} %bitcast.5, bf16[1536,1536]{1,0:T(8,128)(2,1)} %ritz_hbm.1, bf16[4,512,512]{2,1,0:T(8,128)(2,1)} %bitcast.6, s32[4,512]{1,0:T(4,128)} %bitcast.7, s32[4,256]{1,0:T(4,128)} %bitcast.8), custom_call_target="tpu_custom_call" | custom-call | tf_op jit(solution)/shard_map/pallas_call | solution.py:310
  77.3 2.5 %shard_map.56 = bf16[1536,768]{1,0:T(8,128)(2,1)} custom-call(bf16[1536,768]{1,0:T(8,128)(2,1)} %shard_map.55.source), custom_call_target="tpu_custom_call" | custom-call | tf_op jit(solution)/shard_map/pallas_call | solution.py:344
